TPU v7x, 128 devices: a whole 4x4x4 slice. The times are simulated.
128 devices in a mesh: row: 16 (over z, x), col: 8 (over y, core).
Axes of the slice: x: 4, y: 4, z: 4, core: 2. Of those that a mesh axis runs over, the one named last changes fastest.
Arguments:
- edge_vec: float32 [3, 1024], P(None, ('row', 'col')), may hold values from -8 to 8
- edge_atoms: int32 [2, 1024], P(None, ('row', 'col')), may hold values from 0 to 95
- block_weight: bfloat16 [144, 16384], replicated, may hold values from -0.5 to 0.5
- base_hamiltonian: bfloat16 [12288, 12288], P('row', 'col'), as said below
- lower_bound: float32 [1], replicated, may hold values from -50 to -40
- upper_bound: float32 [1], replicated, may hold values from 40 to 50
Outputs:
- purified: float32 [12288, 12288], P('row', 'col')
Inputs may be any that keep to these rules, and one draw needn't show every extreme that they name: `base_hamiltonian`: symmetric.
All inputs are finite; a program needn't handle non-finite values.
Results may differ from a plain program's by a relative error of at most 0.0031.
Values may be sent and summed in bfloat16 or wider, within the bound.
A program may use at most 192 MiB of HBM per device.

v0:
```python
import jax
import jax.numpy as jnp
from jax import lax
from jax.sharding import PartitionSpec as P

ORB = 128
NR = 16
RB = 6


def features(edge_vec):
    squared = jnp.sum(edge_vec * edge_vec, axis=0)
    radius = jnp.sqrt(squared + 0.25)
    unit_x = edge_vec[0] / radius
    unit_y = edge_vec[1] / radius
    unit_z = edge_vec[2] / radius
    harmonics = jnp.stack(
        [
            jnp.ones_like(unit_x),
            unit_x,
            unit_y,
            unit_z,
            unit_x * unit_y,
            unit_y * unit_z,
            unit_z * unit_x,
            unit_x * unit_x - unit_y * unit_y,
            3.0 * unit_z * unit_z - 1.0,
        ]
    )
    centers = 1.0 + 0.3 * jnp.arange(NR, dtype=jnp.float32)
    radial = jnp.exp(-jnp.square((radius[None, :] - centers[:, None]) / 0.5))
    return (radial[:, None, :] * harmonics[None, :, :]).reshape(NR * 9, edge_vec.shape[1])


def shards(edge_vec, edge_atoms, block_weight, base_hamiltonian, lower_bound, upper_bound):
    atoms_float = edge_atoms.astype(jnp.float32)
    packed = jnp.concatenate([features(edge_vec), atoms_float], axis=0)
    gathered = lax.all_gather(packed, ("row", "col"), axis=1, tiled=True)
    embedding = gathered[:-2]
    atom_pairs = gathered[-2:].astype(jnp.int32)
    first_atom = atom_pairs[0]
    second_atom = atom_pairs[1]
    atoms_total = RB * lax.axis_size("row")
    col_blocks = atoms_total // lax.axis_size("col")
    row_index = lax.axis_index("row")
    col_index = lax.axis_index("col")
    row_atoms = row_index * RB + jnp.arange(RB, dtype=jnp.int32)
    col_atoms = col_index * col_blocks + jnp.arange(col_blocks, dtype=jnp.int32)
    direct = (
        (
            (first_atom[None, None, :] == row_atoms[:, None, None])
            & (second_atom[None, None, :] == col_atoms[None, :, None])
        )
        .astype(jnp.float32)
        .reshape(RB * col_blocks, -1)
    )
    mirror = (
        (
            (first_atom[None, None, :] == col_atoms[None, :, None])
            & (second_atom[None, None, :] == row_atoms[:, None, None])
        )
        .astype(jnp.float32)
        .reshape(RB * col_blocks, -1)
    )
    contract = (((1,), (1,)), ((), ()))
    coefficient = lax.dot_general(
        direct, embedding, contract, precision=lax.Precision.HIGHEST
    ).astype(jnp.bfloat16)
    coefficient_back = lax.dot_general(
        mirror, embedding, contract, precision=lax.Precision.HIGHEST
    ).astype(jnp.bfloat16)
    blocks = jnp.dot(coefficient, block_weight, preferred_element_type=jnp.float32).reshape(
        RB, col_blocks, ORB, ORB
    )
    blocks_back = jnp.dot(
        coefficient_back, block_weight, preferred_element_type=jnp.float32
    ).reshape(RB, col_blocks, ORB, ORB)
    tile_rows = RB * ORB
    tile_cols = col_blocks * ORB
    hamiltonian = (
        (blocks + blocks_back.transpose(0, 1, 3, 2))
        .transpose(0, 2, 1, 3)
        .reshape(tile_rows, tile_cols)
    )
    hamiltonian = hamiltonian + base_hamiltonian.astype(jnp.float32)
    global_rows = row_index * tile_rows + jnp.arange(tile_rows, dtype=jnp.int32)
    global_cols = col_index * tile_cols + jnp.arange(tile_cols, dtype=jnp.int32)
    diagonal_mask = global_rows[:, None] == global_cols[None, :]
    shifted = jnp.where(diagonal_mask, upper_bound[0], jnp.float32(0.0)) - hamiltonian
    start_density = (shifted / (upper_bound[0] - lower_bound[0])).astype(jnp.bfloat16)
    row_strip = lax.all_gather(start_density, "col", axis=1, tiled=True)
    return jnp.dot(
        row_strip,
        lax.all_gather(start_density, "row", axis=0, tiled=True),
        preferred_element_type=jnp.float32,
    )


def solution(mesh):
    return jax.shard_map(
        shards,
        mesh=mesh,
        in_specs=(P(None, ("row", "col")), P(None, ("row", "col")), P(), P("row", "col"), P(), P()),
        out_specs=P("row", "col"),
        check_vma=False,
    )
```

profile of v0, /device:TPU:1, one launch (start us, length us, event | category | flops | bytes accessed | tf_op | source)
XLA Modules:
  0.0 437.2 jit_solution(4057055565434168536)
XLA Ops:
  6.5 0.0 all-gather.3.cloned.1.call-start
  6.5 0.7 multiply_reduce_fusion
  7.3 0.8 multiply_subtract_fusion
  9.4 0.8 fusion.6
  10.2 0.1 copy.13
  10.3 0.8 copy.14
  11.1 0.1 negate_exponential_fusion
  11.2 0.1 broadcast_multiply_fusion
  11.3 0.1 mul.81
  11.3 0.1 pad_maximum_fusion
  11.4 39.7 %all_gather.9 = f32[146,1024]{0,1:T(8,128)S(1)} all-gather(f32[146,8]{0,1:T(8,128)S(1)} %pad_maximum_fusion), channel_id=1, replica_groups=mesh['row'=16,'col'=8] {'row','col'}, dimensions={1}, use_global_device_ids=true | all-gather | bytes 602688 | tf_op jit(solution)/shard_map/all_gather | solution.py:38
  51.1 0.2 slice_convert_fusion
  51.3 0.5 slice_reduce_fusion.1
  51.8 0.1 broadcast_compare_fusion.3
  51.9 0.1 broadcast_compare_fusion.1
  52.0 0.1 broadcast_and_fusion
  52.1 0.5 convolution_convert_fusion
  52.7 0.0 slice-start
  52.7 0.5 convolution_convert_fusion.1
  53.2 0.0 slice-start.1
  53.3 3.4 convolution_bitcast_fusion.1
  56.6 3.1 copy.17
  59.7 0.0 slice-done
  59.7 0.0 slice-done.1
  59.7 0.8 convolution_bitcast_fusion
  60.5 3.0 copy.18
  63.5 6.6 %copy.15 = f32[6,12,128,128]{2,1,3,0:T(8,128)} copy(f32[6,12,128,128]{3,2,1,0:T(8,128)} %bitcast.52) | data formatting | bytes 9437184 | tf_op jit(solution)/shard_map/reshape | solution.py:77
  70.1 0.0 copy-start
  70.1 7.3 %bitcast_add_fusion = f32[6,12,128,128]{3,1,2,0:T(8,128)S(1)} fusion(f32[6,12,128,128]{2,1,3,0:T(8,128)} %copy.15, f32[6,12,128,128]{3,2,1,0:T(8,128)} %bitcast.51), kind=kLoop, calls=%fused_computation | loop fusion | flops 1179648 | bytes 14155776 | tf_op jit(solution)/shard_map/add | solution.py:81
  77.3 0.0 copy-done
  77.3 4.2 fusion.2
  81.6 0.0 all-gather.3.cloned.1.call-update
  81.6 0.0 all-gather.5.cloned.1.call-start
  81.6 0.7 all-gather.5.cloned.1.call-update
  82.3 91.0 %all-gather.3.cloned.1.call-done = bf16[768,12288]{1,0:T(8,128)(2,1)} async-done(((bf16[768,1536]{1,0:T(8,128)(2,1)}), bf16[768,12288]{1,0:T(8,128)(2,1)}) %all-gather.3.cloned.1.call-update) | async-done | bytes 18874384 | tf_op jit(solution)/shard_map/all_gather | solution.py:91
  173.4 220.8 %all-gather.5.cloned.1.call-done = bf16[12288,1536]{1,0:T(8,128)(2,1)} async-done(((bf16[768,1536]{1,0:T(8,128)(2,1)}), bf16[12288,1536]{1,0:T(8,128)(2,1)}) %all-gather.5.cloned.1.call-update) | async-done | bytes 37748752 | tf_op jit(solution)/shard_map/all_gather | solution.py:94
  394.2 36.2 %fusion.8 = f32[768,1536]{1,0:T(8,128)} fusion(bf16[768,12288]{1,0:T(8,128)(2,1)} %all-gather.3.cloned.1.call-done, bf16[12288,1536]{1,0:T(8,128)(2,1)} %all-gather.5.cloned.1.call-done), kind=kOutput, calls=%fused_computation.42 | convolution fusion | flops 28991029248 | bytes 61341696 | tf_op jit(solution)/shard_map/dot_general | solution.py:92
  (13 shorter events, 0.2 us)
Async XLA Ops:
  6.5 166.9 %all-gather.3.cloned.1.call-start = ((), (), s32[]{:S(2)}) async-start(), calls=%async_computation | async-start | bytes 21233664 | tf_op jit(solution)/shard_map/all_gather | solution.py:91
  52.7 7.0 %slice-start = ((s8[4718592]{0:T(1024)(128)(4,1)}), s8[4194304]{0:T(1024)(128)(4,1)S(1)}, s32[]{:S(2)}) async-start(s8[4718592]{0:T(1024)(128)(4,1)} %bitcast.49), calls=%async_computation.2 | async-start | bytes 8388608
  53.2 6.5 %slice-start.1 = ((s8[4718592]{0:T(1024)(128)(4,1)}), s8[524288]{0:T(1024)(128)(4,1)S(1)}, s32[]{:S(2)}) async-start(s8[4718592]{0:T(1024)(128)(4,1)} %bitcast.49), calls=%async_computation.3 | async-start | bytes 1048576
  70.1 7.3 %copy-start = (bf16[768,1536]{1,0:T(8,128)(2,1)S(1)}, bf16[768,1536]{1,0:T(8,128)(2,1)}, u32[]{:S(2)}) copy-start(bf16[768,1536]{1,0:T(8,128)(2,1)} %param.9) | copy-start | bytes 7077892
  81.6 312.6 %all-gather.5.cloned.1.call-start = ((), (), s32[]{:S(2)}) async-start(), calls=%async_computation.1 | async-start | bytes 40108032 | tf_op jit(solution)/shard_map/all_gather | solution.py:94
Sparse Core Ops, SparseCore 0:
  81.7 91.6 all-gather.2
  175.5 218.6 all-gather.4
where the time goes:
time: 438 us; the launch traced here: 437 us
  waiting for transfers between devices  313 us (71%)
  matrix products  41.4 us (9%)
  blocking collectives  39.7 us (9%)
  between operations  14.8 us (3%)
  other arithmetic  14.5 us (3%)
  local copies, waits for them, and re-layouts  14.2 us (3%)
    all_gather x1, waiting for transfers between devices, shards(): lax.all_gather(start_density, 'row', axis=0, tiled=True)  221 us
    all_gather x1, waiting for transfers between devices, shards(): row_strip = lax.all_gather(start_density, 'col', axis=1, tiled=True)  91 us
    all_gather x1, blocking collectives, shards(): gathered = lax.all_gather(packed, ('row', 'col'), axis=1, tiled=True)  39.7 us
    dot_general x1, matrix products, shards(): jnp.dot(row_strip, lax.all_gather(start_density, 'row', axis=0, tiled=Tru...  36.2 us
  transfers between devices with their start and end apart: 2, of which 2 were waited for; matrix products, arithmetic and copies ran while one was open for 0% of the time, Pallas kernels for 0%

commit v1 on v0

--- a/solution.py
+++ b/solution.py
@@ -88,7 +88,9 @@
     diagonal_mask = global_rows[:, None] == global_cols[None, :]
     shifted = jnp.where(diagonal_mask, upper_bound[0], jnp.float32(0.0)) - hamiltonian
     start_density = (shifted / (upper_bound[0] - lower_bound[0])).astype(jnp.bfloat16)
-    row_strip = lax.all_gather(start_density, "col", axis=1, tiled=True)
+    row_strip = jnp.concatenate(
+        lax.all_to_all(jnp.stack([start_density] * lax.axis_size("col")), "col", 0, 0), axis=1
+    )
     return jnp.dot(
         row_strip,
         lax.all_gather(start_density, "row", axis=0, tiled=True),

time: 438 us -> 348 us (0.79)
  waiting for transfers between devices: 313 us -> 1.86 us
  blocking collectives: 39.7 us -> 250 us
    all_gather x1, waiting for transfers between devices: 221 us -> 1.85 us  [shards(): lax.all_gather(start_density, 'row', axis=0, tiled=True)]
    all_to_all x0 -> x1, blocking collectives: none -> 210 us  [shards(): lax.all_to_all(jnp.stack([start_density] * lax.axis_size('col')), 'col',...]
    all_gather x1 -> x0, waiting for transfers between devices: 91 us -> none  [shards(): row_strip = lax.all_gather(start_density, 'col', axis=1, tiled=True)]
  transfers between devices with their start and end apart: 2 -> 1, of which waited for: 2 -> 1; matrix products, arithmetic and copies ran while one was open for 0% -> 1% of each run, Pallas kernels for 0% -> 0%
where the time goes in v1:
time: 348 us; the launch traced here: 347 us
  blocking collectives  250 us (72%)
  matrix products  43.8 us (13%)
  other arithmetic  18.8 us (5%)
  local copies, waits for them, and re-layouts  18.4 us (5%)
  between operations  14.8 us (4%)
    all_to_all x1, blocking collectives, shards(): lax.all_to_all(jnp.stack([start_density] * lax.axis_size('col')), 'col',...  210 us
    all_gather x1, blocking collectives, shards(): gathered = lax.all_gather(packed, ('row', 'col'), axis=1, tiled=True)  39.6 us
    dot_general x1, matrix products, shards(): jnp.dot(row_strip, lax.all_gather(start_density, 'row', axis=0, tiled=Tru...  36.5 us
    add x1, other arithmetic, shards(): blocks + blocks_back.transpose(0, 1, 3, 2)  9.91 us
  transfers between devices with their start and end apart: 1, of which 1 were waited for; matrix products, arithmetic and copies ran while one was open for 1% of the time, Pallas kernels for 0%

profile of v1, /device:TPU:1, one launch (start us, length us, event | category | flops | bytes accessed | tf_op | source)
XLA Modules:
  0.0 347.3 jit_solution(12743069790894474994)
XLA Ops:
  6.5 0.0 all-gather.2.cloned.1.call-start
  6.5 0.7 multiply_reduce_fusion
  7.2 0.8 multiply_subtract_fusion
  8.0 0.8 fusion.6
  8.9 0.1 copy.14
  9.0 0.1 negate_exponential_fusion
  9.1 0.1 broadcast_multiply_fusion
  9.2 0.1 mul.81
  9.2 0.8 copy.15
  10.0 0.1 pad_maximum_fusion
  10.1 39.6 %all_gather.6 = f32[146,1024]{0,1:T(8,128)S(1)} all-gather(f32[146,8]{0,1:T(8,128)S(1)} %pad_maximum_fusion), channel_id=1, replica_groups=mesh['row'=16,'col'=8] {'row','col'}, dimensions={1}, use_global_device_ids=true | all-gather | bytes 602688 | tf_op jit(solution)/shard_map/all_gather | solution.py:38
  49.7 0.2 slice_convert_fusion
  49.9 0.5 slice_reduce_fusion.1
  50.5 0.1 broadcast_compare_fusion.1
  50.6 0.1 broadcast_compare_fusion.3
  50.7 0.1 broadcast_and_fusion
  50.8 0.5 convolution_convert_fusion
  51.3 3.1 convolution_bitcast_fusion
  54.5 3.0 copy.20
  57.5 6.6 %copy.16 = f32[6,12,128,128]{2,1,3,0:T(8,128)} copy(f32[6,12,128,128]{3,2,1,0:T(8,128)} %bitcast.54) | data formatting | bytes 9437184 | tf_op jit(solution)/shard_map/reshape | solution.py:77
  64.1 0.5 convolution_convert_fusion.1
  64.7 3.1 convolution_bitcast_fusion.1
  67.8 3.0 copy.19
  72.1 0.0 copy-start
  72.1 9.9 %bitcast_add_fusion = f32[6,12,128,128]{3,1,2,0:T(8,128)} fusion(f32[6,12,128,128]{2,1,3,0:T(8,128)} %copy.16, f32[6,12,128,128]{3,2,1,0:T(8,128)} %bitcast.53), kind=kLoop, calls=%fused_computation | loop fusion | flops 1179648 | bytes 14155776 | tf_op jit(solution)/shard_map/add | solution.py:81
  82.0 0.0 copy-done
  82.0 5.9 %fusion.2 = bf16[768,1536]{1,0:T(8,128)(2,1)} fusion(f32[96,8,12,128]{3,2,1,0:T(8,128)} %bitcast.51, bf16[768,1536]{1,0:T(8,128)(2,1)S(1)} %copy-done, f32[]{:T(128)S(6)} %sub.36, f32[]{:T(128)} %bitcast.49, s32[1536]{0:T(1024)S(1)} %iota_add_fusion, s32[768]{0:T(1024)S(1)} %iota_add_fusion.1), kind=kLoop, calls=%fused_computation.4 | loop fusion | flops 8257536 | bytes 9446408 | tf_op jit(solution)/shard_map/convert_element_type | solution.py:90
  87.9 0.0 all-gather.2.cloned.1.call-update
  87.9 2.8 copy.18
  90.7 1.4 stack.5
  92.2 209.9 %all_to_all.5 = bf16[8,768,1536]{1,2,0:T(8,128)(2,1)} all-to-all(bf16[8,768,1536]{1,2,0:T(8,128)(2,1)S(1)} %stack.5), channel_id=1, replica_groups=mesh['row'=16,'col'=8] {'col'}, dimensions={0} | all-to-all | bytes 37748736 | tf_op jit(solution)/shard_map/all_to_all | solution.py:92
  302.1 1.8 all-gather.2.cloned.1.call-done
  303.9 36.5 %fusion.8 = f32[768,1536]{1,0:T(8,128)} fusion(bf16[768,12288]{0,1:T(8,128)(2,1)} %bitcast.52, bf16[12288,1536]{1,0:T(8,128)(2,1)} %all-gather.2.cloned.1.call-done), kind=kOutput, calls=%fused_computation.42 | convolution fusion | flops 28991029248 | bytes 61341696 | tf_op jit(solution)/shard_map/dot_general | solution.py:94
  (12 shorter events, 0.2 us)
Async XLA Ops:
  6.5 297.4 %all-gather.2.cloned.1.call-start = ((), (), s32[]{:S(2)}) async-start(), calls=%async_computation.1 | async-start | bytes 40108032 | tf_op jit(solution)/shard_map/all_gather | solution.py:96
  72.1 9.9 %copy-start = (bf16[768,1536]{1,0:T(8,128)(2,1)S(1)}, bf16[768,1536]{1,0:T(8,128)(2,1)}, u32[]{:S(2)}) copy-start(bf16[768,1536]{1,0:T(8,128)(2,1)} %param.9) | copy-start | bytes 7077892
Sparse Core Ops, SparseCore 0:
  88.0 215.8 all-gather.1
